TPU v7x, 32 devices: a whole 2x2x4 slice. The times are simulated.
32 devices in a mesh: mom: 4 (over y, x), sec: 8 (over z, core).
Axes of the slice: x: 2, y: 2, z: 4, core: 2. Of those that a mesh axis runs over, the one named last changes fastest.
Arguments:
- left_env: bfloat16 [64, 64, 2816], P('sec', 'mom'), may hold values from -0.75 to 0.75
- right_env: bfloat16 [64, 64, 2816], P('sec', 'mom'), may hold values from -0.109375 to 0.109375
- left_mixed: bfloat16 [4, 64, 64, 2816], P('mom', 'sec'), may hold values from -0.75 to 0.75
- excitation: bfloat16 [4, 64, 64, 256], P('mom', 'sec'), may hold values from -6 to 6
- ground: bfloat16 [64, 64, 256], P('sec'), may hold values from -6 to 6
- mpo: bfloat16 [44, 4, 44, 4], replicated, may hold values from -0.4375 to 0.4375
- momentum: int32 [4], P('mom'), may hold values from 0 to 3, each once
- block_dims: int32 [64], P('sec'), may hold values from 16 to 64, as said below
Outputs:
- excited: bfloat16 [4, 2, 64, 64, 256], P('mom', None, 'sec')
Inputs may be any that keep to these rules, and one draw needn't show every extreme that they name: `block_dims`: every block has at least 16 used rows; some block uses all 64 and some exactly 16.
All inputs are finite; a program needn't handle non-finite values.
Results may differ from a plain program's by a relative error of at most 0.0058.
Values may be sent and summed in bfloat16 or wider, within the bound.
No kernel may reach another device: no remote copies, remote signals or barrier semaphores. Data moves between devices by JAX's collectives and lax.ppermute only.
A program may use at most 128 MiB of HBM per device.

v0:
```python
import math
import jax
import jax.numpy as jnp
from jax import lax
from jax.sharding import PartitionSpec as P


def with_halo(shard, sides, width):
    for axis, dim in sides:
        devices, length = (lax.axis_size(axis), shard.shape[dim])
        up = [(i, (i + 1) % devices) for i in range(devices - 1)]
        down = [(j, i) for i, j in up]
        last = lax.slice_in_dim(shard, length - width, length, axis=dim)
        initial = lax.slice_in_dim(shard, 0, width, axis=dim)
        before = lax.ppermute(last, axis, up)
        after = lax.ppermute(initial, axis, down)
        shard = jnp.concatenate([before, shard, after], axis=dim)
    return shard


def apply_term(left, source, right, mpo):
    width = left.shape[1]
    low = width // 3
    high = width - low
    bounds = [(0, low), (low, high), (high, width)]
    count = source.shape[0]
    rows = left.shape[0]
    block = right.shape[0]
    wide = source.shape[-1]
    phys = wide // block
    total = None
    for shift in range(3):
        start, stop = bounds[shift]
        temp = jnp.einsum(
            "iwa,nab->niwb",
            left[:, start:stop, :],
            source[:, shift],
            preferred_element_type=jnp.float32,
        ).astype(jnp.bfloat16)
        temp = temp.reshape(count, rows, stop - start, phys, block)
        part_sum = jnp.einsum(
            "niwpj,wpvq->nviqj", temp, mpo[start:stop], preferred_element_type=jnp.float32
        )
        total = part_sum if total is None else total + part_sum
    mixed = total.astype(jnp.bfloat16)
    result = jnp.einsum("nviqj,jvk->niqk", mixed, right, preferred_element_type=jnp.float32)
    return result.reshape(count, rows, wide)


def shards(left_env, right_env, left_mixed, excitation, ground, mpo, momentum, block_dims):
    sectors = excitation.shape[1]
    block = excitation.shape[2]
    wide = excitation.shape[3]
    width = left_env.shape[2] // block
    groups = lax.axis_size("mom")
    right_full = lax.all_gather(right_env, "mom", axis=1, tiled=True)
    stacked = jnp.stack([excitation[0], ground])
    padded = with_halo(stacked, (("sec", 1),), 1)
    sector_ids = jnp.arange(sectors, dtype=jnp.int32)

    def shifted_sector(sector):
        right = right_full[sector].reshape(block, width, block)
        mixl = left_mixed[0, sector].reshape(block, width, block)
        src = lax.dynamic_slice_in_dim(padded[1:2], sector, 3, 1)
        return apply_term(mixl, src, right, mpo)[0]

    shifted = lax.map(shifted_sector, sector_ids)
    left_full = lax.all_gather(left_env, "mom", axis=1, tiled=True)

    def direct_sector(sector):
        right = right_full[sector].reshape(block, width, block)
        left = left_full[sector].reshape(block, width, block)
        src = lax.dynamic_slice_in_dim(padded[0:1], sector, 3, 1)
        return apply_term(left, src, right, mpo)[0]

    direct = lax.map(direct_sector, sector_ids)
    phase = 2.0 * math.pi * momentum[0].astype(jnp.float32) / groups
    rows_idx = jnp.arange(block, dtype=jnp.int32)
    cols_idx = jnp.arange(wide, dtype=jnp.int32) % block
    used = block_dims[:, None, None]
    mask = ((rows_idx[None, :, None] < used) & (cols_idx[None, None, :] < used)).astype(jnp.float32)
    real_part = mask * (direct + jnp.cos(phase) * shifted)
    imag_part = -mask * jnp.sin(phase) * shifted
    return jnp.stack([real_part, imag_part])[None].astype(jnp.bfloat16)


def solution(mesh):
    return jax.shard_map(
        shards,
        mesh=mesh,
        in_specs=(
            P("sec", "mom", None),
            P("sec", "mom", None),
            P("mom", "sec", None, None),
            P("mom", "sec", None, None),
            P("sec", None, None),
            P(),
            P("mom"),
            P("sec"),
        ),
        out_specs=P("mom", None, "sec", None, None),
        check_vma=False,
    )
```

profile of v0, /device:TPU:0, one launch (start us, length us, event | category | flops | bytes accessed | tf_op | source)
XLA Modules:
  0.0 640.0 jit_solution(17581412542030367887)
XLA Ops:
  18.7 35.0 %all-gather.3.cloned.1.call-done = bf16[8,64,2816]{2,1,0:T(8,128)(2,1)} async-done(((bf16[8,16,2816]{2,1,0:T(8,128)(2,1)}), bf16[8,64,2816]{2,1,0:T(8,128)(2,1)}) %all-gather.3.cloned.1.call-update) | async-done | bytes 2883600 | tf_op jit(solution)/shard_map/all_gather | solution.py:68
  53.7 43.7 %all-gather.5.cloned.1.call-done = bf16[8,64,2816]{2,1,0:T(8,128)(2,1)} async-done(((bf16[8,16,2816]{2,1,0:T(8,128)(2,1)}), bf16[8,64,2816]{2,1,0:T(8,128)(2,1)}) %all-gather.5.cloned.1.call-update) | async-done | bytes 2883600 | tf_op jit(solution)/shard_map/all_gather | solution.py:56
  98.3 268.4 %while.20 = (s32[]{:T(128)}, f32[8,64,256]{2,1,0:T(8,128)}, bf16[2,10,64,256]{3,2,1,0:T(8,128)(2,1)S(1)}, s32[8]{0:T(128)S(1)}, bf16[8,64,2816]{2,1,0:T(8,128)(2...) while((s32[]{:T(128)}, f32[8,64,256]{2,1,0:T(8,128)}, ...), condition=%wide.region_1.2_spmd, body=%wide.region_0.1_spmd.sunk | while | flops 441188352 | bytes 44241284 | solution.py:76
  104.7 3.7 fusion.105
  115.9 6.3 fusion.110
  122.3 5.2 copy.125
  138.2 3.7 fusion.105
  143.5 3.7 fusion.108
  149.5 6.3 fusion.110
  155.8 5.2 copy.125
  171.8 3.7 fusion.105
  177.0 3.7 fusion.108
  183.0 6.3 fusion.110
  189.4 5.2 copy.125
  205.3 3.7 fusion.105
  210.6 3.7 fusion.108
  216.6 6.3 fusion.110
  222.9 5.2 copy.125
  238.9 3.7 fusion.105
  244.1 3.7 fusion.108
  250.1 6.3 fusion.110
  256.5 5.2 copy.125
  272.5 3.7 fusion.105
  277.7 3.7 fusion.108
  283.7 6.3 fusion.110
  290.0 5.2 copy.125
  306.0 3.7 fusion.105
  311.2 3.7 fusion.108
  317.3 6.3 fusion.110
  323.6 5.2 copy.125
  339.6 3.7 fusion.105
  344.8 3.7 fusion.108
  350.8 6.3 fusion.110
  357.2 5.2 copy.125
  367.5 263.4 %while.21 = (s32[]{:T(128)}, f32[8,64,256]{2,1,0:T(8,128)}, bf16[2,10,64,256]{3,2,1,0:T(8,128)(2,1)S(1)}, s32[8]{0:T(128)S(1)}, bf16[1,8,64,2816]{3,2,1,0:T(8,12...) while((s32[]{:T(128)}, f32[8,64,256]{2,1,0:T(8,128)}, ...), condition=%wide.region_3.4_spmd, body=%wide.region_2.3_spmd.sunk | while | flops 441188352 | bytes 43225452 | solution.py:67
  373.8 3.7 fusion.123
  378.2 3.7 fusion.126
  383.5 6.3 fusion.128
  389.8 5.2 copy.133
  406.7 3.7 fusion.123
  411.2 3.7 fusion.126
  416.4 6.3 fusion.128
  422.8 5.2 copy.133
  439.6 3.7 fusion.123
  444.1 3.7 fusion.126
  449.3 6.3 fusion.128
  455.7 5.2 copy.133
  472.5 3.7 fusion.123
  482.3 6.3 fusion.128
  488.6 5.2 copy.133
  505.5 3.7 fusion.123
  515.2 6.3 fusion.128
  521.5 5.2 copy.133
  538.4 3.7 fusion.123
  542.9 3.7 fusion.126
  548.1 6.3 fusion.128
  554.5 5.2 copy.133
  571.3 3.7 fusion.123
  581.1 6.3 fusion.128
  587.4 5.2 copy.133
  604.3 3.7 fusion.123
  608.8 3.7 fusion.126
  614.0 6.3 fusion.128
  620.3 5.2 copy.133
  (452 shorter events, 205.8 us)
Async XLA Ops:
  6.5 47.2 %all-gather.3.cloned.1.call-start = ((), (), s32[]{:S(2)}) async-start(), calls=%async_computation | async-start | bytes 3604480 | tf_op jit(solution)/shard_map/all_gather | solution.py:68
  7.3 90.2 %all-gather.5.cloned.1.call-start = ((), (), s32[]{:S(2)}) async-start(), calls=%async_computation.1 | async-start | bytes 3604480 | tf_op jit(solution)/shard_map/all_gather | solution.py:56
  8.8 8.7 %collective-permute-start.1 = (bf16[2,1,64,256]{3,2,1,0:T(8,128)(2,1)S(1)}, bf16[2,1,64,256]{3,2,1,0:T(8,128)(2,1)S(1)}, u32[]{:S(2)}, u32[]{:S(2)}) collective-permute-start(bf16[2,1,64,256]{3,2,1,0:T(8,128)(2,1)S(1)} %get-tuple-element.146), channel_id=1, source_target_pairs={{1,0},{2,1},{3,2},{4,3},{5,4},{6,5},{7,6},{9,8},{10,9},{11,10},{12... | collective-permute-start | bytes 196616 | tf_op jit(solution)/shard_map/ppermute | solution.py:16
  10.1 7.4 %collective-permute-start = (bf16[2,1,64,256]{3,2,1,0:T(8,128)(2,1)S(1)}, bf16[2,1,64,256]{3,2,1,0:T(8,128)(2,1)S(1)}, u32[]{:S(2)}, u32[]{:S(2)}) collective-permute-start(bf16[2,1,64,256]{3,2,1,0:T(8,128)(2,1)S(1)} %get-tuple-element.145), channel_id=1, source_target_pairs={{0,1},{1,2},{2,3},{3,4},{4,5},{5,6},{6,7},{8,9},{9,10},{10,11},{11... | collective-permute-start | bytes 196616 | tf_op jit(solution)/shard_map/ppermute | solution.py:15
  98.3 5.7 copy-start.4
  98.3 11.6 %copy-start = (bf16[44,4,44,4]{2,0,1,3:T(8,128)(2,1)}, bf16[44,4,44,4]{2,0,1,3:T(8,128)(2,1)S(1)}, u32[]{:S(2)}) copy-start(bf16[44,4,44,4]{2,0,1,3:T(8,128)(2,1)S(1)} %get-tuple-element.276) | copy-start | bytes 185860 | tf_op jit(solution)/shard_map/while
  127.5 4.3 copy-start.1
  127.5 4.3 copy-start.5
  131.8 5.7 copy-start.4
  131.8 11.6 %copy-start = (bf16[44,4,44,4]{2,0,1,3:T(8,128)(2,1)}, bf16[44,4,44,4]{2,0,1,3:T(8,128)(2,1)S(1)}, u32[]{:S(2)}) copy-start(bf16[44,4,44,4]{2,0,1,3:T(8,128)(2,1)S(1)} %get-tuple-element.276) | copy-start | bytes 185860 | tf_op jit(solution)/shard_map/while
  161.0 4.3 copy-start.1
  161.0 4.3 copy-start.5
  165.4 5.7 copy-start.4
  165.4 11.6 %copy-start = (bf16[44,4,44,4]{2,0,1,3:T(8,128)(2,1)}, bf16[44,4,44,4]{2,0,1,3:T(8,128)(2,1)S(1)}, u32[]{:S(2)}) copy-start(bf16[44,4,44,4]{2,0,1,3:T(8,128)(2,1)S(1)} %get-tuple-element.276) | copy-start | bytes 185860 | tf_op jit(solution)/shard_map/while
  194.6 4.3 copy-start.1
  194.6 4.3 copy-start.5
  198.9 5.7 copy-start.4
  198.9 11.6 %copy-start = (bf16[44,4,44,4]{2,0,1,3:T(8,128)(2,1)}, bf16[44,4,44,4]{2,0,1,3:T(8,128)(2,1)S(1)}, u32[]{:S(2)}) copy-start(bf16[44,4,44,4]{2,0,1,3:T(8,128)(2,1)S(1)} %get-tuple-element.276) | copy-start | bytes 185860 | tf_op jit(solution)/shard_map/while
  228.2 4.3 copy-start.1
  228.2 4.3 copy-start.5
  232.5 5.7 copy-start.4
  232.5 11.6 %copy-start = (bf16[44,4,44,4]{2,0,1,3:T(8,128)(2,1)}, bf16[44,4,44,4]{2,0,1,3:T(8,128)(2,1)S(1)}, u32[]{:S(2)}) copy-start(bf16[44,4,44,4]{2,0,1,3:T(8,128)(2,1)S(1)} %get-tuple-element.276) | copy-start | bytes 185860 | tf_op jit(solution)/shard_map/while
  261.7 4.3 copy-start.1
  261.7 4.3 copy-start.5
  266.0 5.7 copy-start.4
  266.0 11.6 %copy-start = (bf16[44,4,44,4]{2,0,1,3:T(8,128)(2,1)}, bf16[44,4,44,4]{2,0,1,3:T(8,128)(2,1)S(1)}, u32[]{:S(2)}) copy-start(bf16[44,4,44,4]{2,0,1,3:T(8,128)(2,1)S(1)} %get-tuple-element.276) | copy-start | bytes 185860 | tf_op jit(solution)/shard_map/while
  295.3 4.3 copy-start.5
  299.6 5.7 copy-start.4
  299.6 11.6 %copy-start = (bf16[44,4,44,4]{2,0,1,3:T(8,128)(2,1)}, bf16[44,4,44,4]{2,0,1,3:T(8,128)(2,1)S(1)}, u32[]{:S(2)}) copy-start(bf16[44,4,44,4]{2,0,1,3:T(8,128)(2,1)S(1)} %get-tuple-element.276) | copy-start | bytes 185860 | tf_op jit(solution)/shard_map/while
  328.8 4.3 copy-start.5
  333.1 5.7 copy-start.4
  333.2 11.6 %copy-start = (bf16[44,4,44,4]{2,0,1,3:T(8,128)(2,1)}, bf16[44,4,44,4]{2,0,1,3:T(8,128)(2,1)S(1)}, u32[]{:S(2)}) copy-start(bf16[44,4,44,4]{2,0,1,3:T(8,128)(2,1)S(1)} %get-tuple-element.276) | copy-start | bytes 185860 | tf_op jit(solution)/shard_map/while
  362.4 4.3 copy-start.1
  362.4 4.3 copy-start.5
  367.5 263.4 %copy-start.9 = (pred[8,256]{1,0:T(8,128)(4,1)S(1)}, pred[8,256]{1,0:T(8,128)(4,1)}, u32[]{:S(2)}) copy-start(pred[8,256]{1,0:T(8,128)(4,1)} %broadcast_compare_fusion) | copy-start | bytes 6148
  367.5 263.4 %copy-start.10 = (pred[8,64]{1,0:T(8,128)(4,1)S(1)}, pred[8,64]{1,0:T(8,128)(4,1)}, u32[]{:S(2)}) copy-start(pred[8,64]{1,0:T(8,128)(4,1)} %iota_compare_fusion) | copy-start | bytes 1540
  367.5 5.5 copy-start.6
  367.5 10.7 %copy-start.2 = (bf16[44,4,44,4]{2,0,1,3:T(8,128)(2,1)}, bf16[44,4,44,4]{2,0,1,3:T(8,128)(2,1)S(1)}, u32[]{:S(2)}) copy-start(bf16[44,4,44,4]{2,0,1,3:T(8,128)(2,1)S(1)} %get-tuple-element.315) | copy-start | bytes 185860 | tf_op jit(solution)/shard_map/while
  396.1 4.3 copy-start.3
  400.4 5.6 copy-start.6
  400.4 10.8 %copy-start.2 = (bf16[44,4,44,4]{2,0,1,3:T(8,128)(2,1)}, bf16[44,4,44,4]{2,0,1,3:T(8,128)(2,1)S(1)}, u32[]{:S(2)}) copy-start(bf16[44,4,44,4]{2,0,1,3:T(8,128)(2,1)S(1)} %get-tuple-element.315) | copy-start | bytes 185860 | tf_op jit(solution)/shard_map/while
  429.0 4.3 copy-start.3
  433.3 5.6 copy-start.6
  433.3 10.8 %copy-start.2 = (bf16[44,4,44,4]{2,0,1,3:T(8,128)(2,1)}, bf16[44,4,44,4]{2,0,1,3:T(8,128)(2,1)S(1)}, u32[]{:S(2)}) copy-start(bf16[44,4,44,4]{2,0,1,3:T(8,128)(2,1)S(1)} %get-tuple-element.315) | copy-start | bytes 185860 | tf_op jit(solution)/shard_map/while
  461.9 4.3 copy-start.3
  466.2 5.6 copy-start.6
  466.2 10.8 %copy-start.2 = (bf16[44,4,44,4]{2,0,1,3:T(8,128)(2,1)}, bf16[44,4,44,4]{2,0,1,3:T(8,128)(2,1)S(1)}, u32[]{:S(2)}) copy-start(bf16[44,4,44,4]{2,0,1,3:T(8,128)(2,1)S(1)} %get-tuple-element.315) | copy-start | bytes 185860 | tf_op jit(solution)/shard_map/while
  494.8 4.3 copy-start.3
  499.2 5.6 copy-start.6
  499.2 10.8 %copy-start.2 = (bf16[44,4,44,4]{2,0,1,3:T(8,128)(2,1)}, bf16[44,4,44,4]{2,0,1,3:T(8,128)(2,1)S(1)}, u32[]{:S(2)}) copy-start(bf16[44,4,44,4]{2,0,1,3:T(8,128)(2,1)S(1)} %get-tuple-element.315) | copy-start | bytes 185860 | tf_op jit(solution)/shard_map/while
  527.8 4.3 copy-start.3
  527.8 4.3 copy-start.7
  532.1 5.6 copy-start.6
  532.1 10.8 %copy-start.2 = (bf16[44,4,44,4]{2,0,1,3:T(8,128)(2,1)}, bf16[44,4,44,4]{2,0,1,3:T(8,128)(2,1)S(1)}, u32[]{:S(2)}) copy-start(bf16[44,4,44,4]{2,0,1,3:T(8,128)(2,1)S(1)} %get-tuple-element.315) | copy-start | bytes 185860 | tf_op jit(solution)/shard_map/while
  560.7 4.3 copy-start.3
  560.7 4.3 copy-start.7
  565.0 5.6 copy-start.6
  565.0 10.8 %copy-start.2 = (bf16[44,4,44,4]{2,0,1,3:T(8,128)(2,1)}, bf16[44,4,44,4]{2,0,1,3:T(8,128)(2,1)S(1)}, u32[]{:S(2)}) copy-start(bf16[44,4,44,4]{2,0,1,3:T(8,128)(2,1)S(1)} %get-tuple-element.315) | copy-start | bytes 185860 | tf_op jit(solution)/shard_map/while
  593.7 4.3 copy-start.3
  593.7 4.3 copy-start.7
  598.0 5.6 copy-start.6
  598.0 10.8 %copy-start.2 = (bf16[44,4,44,4]{2,0,1,3:T(8,128)(2,1)}, bf16[44,4,44,4]{2,0,1,3:T(8,128)(2,1)S(1)}, u32[]{:S(2)}) copy-start(bf16[44,4,44,4]{2,0,1,3:T(8,128)(2,1)S(1)} %get-tuple-element.315) | copy-start | bytes 185860 | tf_op jit(solution)/shard_map/while
  626.6 4.3 copy-start.3
  626.6 4.3 copy-start.7
  (14 other events, 41.6 us)
Sparse Core Ops, SparseCore 0:
  9.2 44.4 all-gather.2
  55.6 41.7 all-gather.4
where the time goes:
time: 643 us; the launch traced here: 640 us
  matrix products  291 us (45%)
  local copies, waits for them, and re-layouts  191 us (30%)
  waiting for transfers between devices  80.1 us (12%)
  loops' own time  52.6 us (8%)
  between operations  14.3 us (2%)
  other arithmetic  6.82 us (1%)
    dot_general x48, matrix products, apply_term(): jnp.einsum('niwpj,wpvq->nviqj', temp, mpo[start:stop], preferred_element_...  220 us
    another operation x66, local copies, waits for them, and re-layouts  119 us
    dot_general x16, matrix products, apply_term(): jnp.einsum('nviqj,jvk->niqk', mixed, right, preferred_element_type=jnp.fl...  46.1 us
    all_gather x1, waiting for transfers between devices, shards(): right_full = lax.all_gather(right_env, 'mom', axis=1, tiled=True)  43.7 us
    all_gather x1, waiting for transfers between devices, shards(): left_full = lax.all_gather(left_env, 'mom', axis=1, tiled=True)  35 us
    another operation x1, loops' own time, shards(): shifted = lax.map(shifted_sector, sector_ids)  26.6 us
    another operation x1, loops' own time, shards(): direct = lax.map(direct_sector, sector_ids)  26 us
    dot_general x48, matrix products, apply_term(): jnp.einsum('iwa,nab->niwb', left[:, start:stop, :], source[:, shift], pre...  25 us
  transfers between devices with their start and end apart: 4, of which 2 were waited for; matrix products, arithmetic and copies ran while one was open for 1% of the time, Pallas kernels for 0%

commit v1 on v0

--- a/solution.py
+++ b/solution.py
@@ -53,7 +53,12 @@
     wide = excitation.shape[3]
     width = left_env.shape[2] // block
     groups = lax.axis_size("mom")
-    right_full = lax.all_gather(right_env, "mom", axis=1, tiled=True)
+    ring = [right_env]
+    for hop in range(3):
+        ring.append(lax.ppermute(ring[-1], "mom", [(dev, (dev + 1) % 4) for dev in range(4)]))
+    right_full = jnp.roll(
+        jnp.concatenate(ring[::-1], axis=1), (lax.axis_index("mom") + 1) * ring[0].shape[1], axis=1
+    )
     stacked = jnp.stack([excitation[0], ground])
     padded = with_halo(stacked, (("sec", 1),), 1)
     sector_ids = jnp.arange(sectors, dtype=jnp.int32)

time: 643 us -> 630 us (0.980)
  waiting for transfers between devices: 80.1 us -> 40.9 us
  matrix products: 291 us -> 306 us
    all_gather x1 -> x0, waiting for transfers between devices: 43.7 us -> none  [shards(): right_full = lax.all_gather(right_env, 'mom', axis=1, tiled=True)]
    ppermute x0 -> x3, waiting for transfers between devices: none -> 40.9 us  [shards(): lax.ppermute(ring[-1], 'mom', [(dev, (dev + 1) % 4) for dev in range(4)])]
    all_gather x1, waiting for transfers between devices: 35 us -> 0.01 us  [shards(): left_full = lax.all_gather(left_env, 'mom', axis=1, tiled=True)]
    dot_general x48, matrix products: 220 us -> 247 us  [apply_term(): jnp.einsum('niwpj,wpvq->nviqj', temp, mpo[start:stop], preferred_element_...]
    dot_general x48, matrix products: 25 us -> 12.9 us  [apply_term(): jnp.einsum('iwa,nab->niwb', left[:, start:stop, :], source[:, shift], pre...]
  transfers between devices with their start and end apart: 4 -> 6, of which waited for: 2 -> 3; matrix products, arithmetic and copies ran while one was open for 1% -> 42% of each run, Pallas kernels for 0% -> 0%
where the time goes in v1:
time: 630 us; the launch traced here: 626 us
  matrix products  306 us (49%)
  local copies, waits for them, and re-layouts  197 us (31%)
  loops' own time  52.6 us (8%)
  waiting for transfers between devices  40.9 us (6%)
  between operations  14.3 us (2%)
  starting transfers between devices  7.99 us (1%)
  other arithmetic  6.86 us (1%)
    dot_general x48, matrix products, apply_term(): jnp.einsum('niwpj,wpvq->nviqj', temp, mpo[start:stop], preferred_element_...  247 us
    another operation x66, local copies, waits for them, and re-layouts  118 us
    dot_general x16, matrix products, apply_term(): jnp.einsum('nviqj,jvk->niqk', mixed, right, preferred_element_type=jnp.fl...  46.1 us
    ppermute x3, waiting for transfers between devices, shards(): lax.ppermute(ring[-1], 'mom', [(dev, (dev + 1) % 4) for dev in range(4)])  40.9 us
    another operation x1, loops' own time, shards(): shifted = lax.map(shifted_sector, sector_ids)  26.3 us
    another operation x1, loops' own time, shards(): direct = lax.map(direct_sector, sector_ids)  26.3 us
    dot_general x48, matrix products, apply_term(): jnp.einsum('iwa,nab->niwb', left[:, start:stop, :], source[:, shift], pre...  12.9 us
  transfers between devices with their start and end apart: 6, of which 3 were waited for; matrix products, arithmetic and copies ran while one was open for 42% of the time, Pallas kernels for 0%

profile of v1, /device:TPU:0, one launch (start us, length us, event | category | flops | bytes accessed | tf_op | source)
XLA Modules:
  0.0 626.0 jit_solution(1470597375782306989)
XLA Ops:
  9.5 17.4 %collective-permute-done.2 = bf16[8,16,2816]{2,1,0:T(8,128)(2,1)S(1)} collective-permute-done((bf16[8,16,2816]{2,1,0:T(8,128)(2,1)}, bf16[8,16,2816]{2,1,0:T(8,128)(2,1)S(1)}, u32[]{:S(2)}, u32[]{:S(2)}) %collective-permute-start.2) | collective-permute-done | bytes 720928 | tf_op jit(solution)/shard_map/ppermute | solution.py:58
  27.6 17.5 %collective-permute-done.3 = bf16[8,16,2816]{2,1,0:T(8,128)(2,1)S(1)} collective-permute-done((bf16[8,16,2816]{2,1,0:T(8,128)(2,1)S(1)}, bf16[8,16,2816]{2,1,0:T(8,128)(2,1)S(1)}, u32[]{:S(2)}, u32[]{:S(2)}) %collective-permute-start.3) | collective-permute-done | bytes 720928 | tf_op jit(solution)/shard_map/ppermute | solution.py:58
  56.5 6.0 collective-permute-done.4
  67.8 277.9 %while.21 = (s32[]{:T(128)}, f32[8,64,256]{2,1,0:T(8,128)}, bf16[2,10,64,256]{3,2,1,0:T(8,128)(2,1)S(1)}, s32[8]{0:T(128)S(1)}, bf16[1,8,64,2816]{3,2,1,0:T(8,12...) while((s32[]{:T(128)}, f32[8,64,256]{2,1,0:T(8,128)}, ...), condition=%wide.region_3.4_spmd, body=%wide.region_2.3_spmd.sunk | while | flops 441188352 | bytes 41746740 | solution.py:72
  74.1 4.6 fusion.123
  79.5 4.5 fusion.126
  85.6 6.3 %fusion.128 = bf16[44,64,4,64]{3,0,2,1:T(8,128)(2,1)S(1)} fusion(f32[64,64,44,4,1]{1,2,4,3,0:T(8,128)} %fusion.123, f32[64,64,44,4,1]{1,2,4,3,0:T(8,128)} %fusion.126, bf16[64,14,4,64,1]{3,2,0,1,4:T(4,128)(2,1)} %bitcast.261, bf16[44,4,44,4]{2,0,1,3:T(8,128)(2,1)} %get-tuple-element.315), kind=kOutput, calls=%fused_computation.38.clone.1 | convolution fusion | flops 82903040 | bytes 15007744 | tf_op jit(solution)/shard_map/while/body/eval_jaxpr/niwpj,wpvq->nviqj/dot_general | solution.py:41
  91.9 5.2 copy.133
  108.9 4.6 fusion.123
  114.2 4.5 fusion.126
  120.3 6.3 %fusion.128 = bf16[44,64,4,64]{3,0,2,1:T(8,128)(2,1)S(1)} fusion(f32[64,64,44,4,1]{1,2,4,3,0:T(8,128)} %fusion.123, f32[64,64,44,4,1]{1,2,4,3,0:T(8,128)} %fusion.126, bf16[64,14,4,64,1]{3,2,0,1,4:T(4,128)(2,1)} %bitcast.261, bf16[44,4,44,4]{2,0,1,3:T(8,128)(2,1)} %get-tuple-element.315), kind=kOutput, calls=%fused_computation.38.clone.1 | convolution fusion | flops 82903040 | bytes 15007744 | tf_op jit(solution)/shard_map/while/body/eval_jaxpr/niwpj,wpvq->nviqj/dot_general | solution.py:41
  126.7 5.2 copy.133
  143.6 4.6 fusion.123
  149.0 4.5 fusion.126
  155.0 6.3 %fusion.128 = bf16[44,64,4,64]{3,0,2,1:T(8,128)(2,1)S(1)} fusion(f32[64,64,44,4,1]{1,2,4,3,0:T(8,128)} %fusion.123, f32[64,64,44,4,1]{1,2,4,3,0:T(8,128)} %fusion.126, bf16[64,14,4,64,1]{3,2,0,1,4:T(4,128)(2,1)} %bitcast.261, bf16[44,4,44,4]{2,0,1,3:T(8,128)(2,1)} %get-tuple-element.315), kind=kOutput, calls=%fused_computation.38.clone.1 | convolution fusion | flops 82903040 | bytes 15007744 | tf_op jit(solution)/shard_map/while/body/eval_jaxpr/niwpj,wpvq->nviqj/dot_general | solution.py:41
  161.4 5.2 copy.133
  178.3 4.6 fusion.123
  183.7 4.5 fusion.126
  189.8 6.3 %fusion.128 = bf16[44,64,4,64]{3,0,2,1:T(8,128)(2,1)S(1)} fusion(f32[64,64,44,4,1]{1,2,4,3,0:T(8,128)} %fusion.123, f32[64,64,44,4,1]{1,2,4,3,0:T(8,128)} %fusion.126, bf16[64,14,4,64,1]{3,2,0,1,4:T(4,128)(2,1)} %bitcast.261, bf16[44,4,44,4]{2,0,1,3:T(8,128)(2,1)} %get-tuple-element.315), kind=kOutput, calls=%fused_computation.38.clone.1 | convolution fusion | flops 82903040 | bytes 15007744 | tf_op jit(solution)/shard_map/while/body/eval_jaxpr/niwpj,wpvq->nviqj/dot_general | solution.py:41
  196.1 5.2 copy.133
  213.1 4.6 fusion.123
  218.4 4.5 fusion.126
  224.5 6.3 %fusion.128 = bf16[44,64,4,64]{3,0,2,1:T(8,128)(2,1)S(1)} fusion(f32[64,64,44,4,1]{1,2,4,3,0:T(8,128)} %fusion.123, f32[64,64,44,4,1]{1,2,4,3,0:T(8,128)} %fusion.126, bf16[64,14,4,64,1]{3,2,0,1,4:T(4,128)(2,1)} %bitcast.261, bf16[44,4,44,4]{2,0,1,3:T(8,128)(2,1)} %get-tuple-element.315), kind=kOutput, calls=%fused_computation.38.clone.1 | convolution fusion | flops 82903040 | bytes 15007744 | tf_op jit(solution)/shard_map/while/body/eval_jaxpr/niwpj,wpvq->nviqj/dot_general | solution.py:41
  230.9 5.2 copy.133
  247.8 4.6 fusion.123
  253.2 4.5 fusion.126
  259.3 6.3 %fusion.128 = bf16[44,64,4,64]{3,0,2,1:T(8,128)(2,1)S(1)} fusion(f32[64,64,44,4,1]{1,2,4,3,0:T(8,128)} %fusion.123, f32[64,64,44,4,1]{1,2,4,3,0:T(8,128)} %fusion.126, bf16[64,14,4,64,1]{3,2,0,1,4:T(4,128)(2,1)} %bitcast.261, bf16[44,4,44,4]{2,0,1,3:T(8,128)(2,1)} %get-tuple-element.315), kind=kOutput, calls=%fused_computation.38.clone.1 | convolution fusion | flops 82903040 | bytes 15007744 | tf_op jit(solution)/shard_map/while/body/eval_jaxpr/niwpj,wpvq->nviqj/dot_general | solution.py:41
  265.6 5.2 copy.133
  282.5 4.6 fusion.123
  294.0 6.3 %fusion.128 = bf16[44,64,4,64]{3,0,2,1:T(8,128)(2,1)S(1)} fusion(f32[64,64,44,4,1]{1,2,4,3,0:T(8,128)} %fusion.123, f32[64,64,44,4,1]{1,2,4,3,0:T(8,128)} %fusion.126, bf16[64,14,4,64,1]{3,2,0,1,4:T(4,128)(2,1)} %bitcast.261, bf16[44,4,44,4]{2,0,1,3:T(8,128)(2,1)} %get-tuple-element.315), kind=kOutput, calls=%fused_computation.38.clone.1 | convolution fusion | flops 82903040 | bytes 15007744 | tf_op jit(solution)/shard_map/while/body/eval_jaxpr/niwpj,wpvq->nviqj/dot_general | solution.py:41
  300.3 5.2 copy.133
  317.3 4.6 fusion.123
  322.7 4.5 fusion.126
  328.7 6.3 %fusion.128 = bf16[44,64,4,64]{3,0,2,1:T(8,128)(2,1)S(1)} fusion(f32[64,64,44,4,1]{1,2,4,3,0:T(8,128)} %fusion.123, f32[64,64,44,4,1]{1,2,4,3,0:T(8,128)} %fusion.126, bf16[64,14,4,64,1]{3,2,0,1,4:T(4,128)(2,1)} %bitcast.261, bf16[44,4,44,4]{2,0,1,3:T(8,128)(2,1)} %get-tuple-element.315), kind=kOutput, calls=%fused_computation.38.clone.1 | convolution fusion | flops 82903040 | bytes 15007744 | tf_op jit(solution)/shard_map/while/body/eval_jaxpr/niwpj,wpvq->nviqj/dot_general | solution.py:41
  335.1 5.2 copy.133
  346.5 270.3 %while.20 = (s32[]{:T(128)}, f32[8,64,256]{2,1,0:T(8,128)}, bf16[2,10,64,256]{3,2,1,0:T(8,128)(2,1)S(1)}, s32[8]{0:T(128)S(1)}, bf16[8,64,2816]{2,1,0:T(8,128)(2...) while((s32[]{:T(128)}, f32[8,64,256]{2,1,0:T(8,128)}, ...), condition=%wide.region_1.2_spmd, body=%wide.region_0.1_spmd.sunk | while | flops 441188352 | bytes 41746736 | solution.py:81
  352.9 4.6 fusion.105
  364.3 6.3 %fusion.110 = bf16[44,64,4,64]{3,0,2,1:T(8,128)(2,1)S(1)} fusion(f32[64,64,44,4,1]{1,2,4,3,0:T(8,128)} %fusion.105, f32[64,64,44,4,1]{1,2,4,3,0:T(8,128)} %fusion.108, bf16[64,14,4,64,1]{3,2,0,1,4:T(4,128)(2,1)} %bitcast.262, bf16[44,4,44,4]{2,0,1,3:T(8,128)(2,1)} %get-tuple-element.276), kind=kOutput, calls=%fused_computation.3.clone.1 | convolution fusion | flops 82903040 | bytes 15007744 | tf_op jit(solution)/shard_map/while/body/eval_jaxpr/niwpj,wpvq->nviqj/dot_general | solution.py:41
  370.7 5.2 copy.125
  386.7 4.6 fusion.105
  392.1 4.5 fusion.108
  398.1 6.3 %fusion.110 = bf16[44,64,4,64]{3,0,2,1:T(8,128)(2,1)S(1)} fusion(f32[64,64,44,4,1]{1,2,4,3,0:T(8,128)} %fusion.105, f32[64,64,44,4,1]{1,2,4,3,0:T(8,128)} %fusion.108, bf16[64,14,4,64,1]{3,2,0,1,4:T(4,128)(2,1)} %bitcast.262, bf16[44,4,44,4]{2,0,1,3:T(8,128)(2,1)} %get-tuple-element.276), kind=kOutput, calls=%fused_computation.3.clone.1 | convolution fusion | flops 82903040 | bytes 15007744 | tf_op jit(solution)/shard_map/while/body/eval_jaxpr/niwpj,wpvq->nviqj/dot_general | solution.py:41
  404.5 5.2 copy.125
  420.5 4.6 fusion.105
  432.0 6.3 %fusion.110 = bf16[44,64,4,64]{3,0,2,1:T(8,128)(2,1)S(1)} fusion(f32[64,64,44,4,1]{1,2,4,3,0:T(8,128)} %fusion.105, f32[64,64,44,4,1]{1,2,4,3,0:T(8,128)} %fusion.108, bf16[64,14,4,64,1]{3,2,0,1,4:T(4,128)(2,1)} %bitcast.262, bf16[44,4,44,4]{2,0,1,3:T(8,128)(2,1)} %get-tuple-element.276), kind=kOutput, calls=%fused_computation.3.clone.1 | convolution fusion | flops 82903040 | bytes 15007744 | tf_op jit(solution)/shard_map/while/body/eval_jaxpr/niwpj,wpvq->nviqj/dot_general | solution.py:41
  438.3 5.2 copy.125
  454.3 4.6 fusion.105
  459.7 4.5 fusion.108
  465.8 6.3 %fusion.110 = bf16[44,64,4,64]{3,0,2,1:T(8,128)(2,1)S(1)} fusion(f32[64,64,44,4,1]{1,2,4,3,0:T(8,128)} %fusion.105, f32[64,64,44,4,1]{1,2,4,3,0:T(8,128)} %fusion.108, bf16[64,14,4,64,1]{3,2,0,1,4:T(4,128)(2,1)} %bitcast.262, bf16[44,4,44,4]{2,0,1,3:T(8,128)(2,1)} %get-tuple-element.276), kind=kOutput, calls=%fused_computation.3.clone.1 | convolution fusion | flops 82903040 | bytes 15007744 | tf_op jit(solution)/shard_map/while/body/eval_jaxpr/niwpj,wpvq->nviqj/dot_general | solution.py:41
  472.1 5.2 copy.125
  488.1 4.6 fusion.105
  499.6 6.3 %fusion.110 = bf16[44,64,4,64]{3,0,2,1:T(8,128)(2,1)S(1)} fusion(f32[64,64,44,4,1]{1,2,4,3,0:T(8,128)} %fusion.105, f32[64,64,44,4,1]{1,2,4,3,0:T(8,128)} %fusion.108, bf16[64,14,4,64,1]{3,2,0,1,4:T(4,128)(2,1)} %bitcast.262, bf16[44,4,44,4]{2,0,1,3:T(8,128)(2,1)} %get-tuple-element.276), kind=kOutput, calls=%fused_computation.3.clone.1 | convolution fusion | flops 82903040 | bytes 15007744 | tf_op jit(solution)/shard_map/while/body/eval_jaxpr/niwpj,wpvq->nviqj/dot_general | solution.py:41
  505.9 5.2 copy.125
  521.9 4.6 fusion.105
  527.3 4.5 fusion.108
  533.4 6.3 %fusion.110 = bf16[44,64,4,64]{3,0,2,1:T(8,128)(2,1)S(1)} fusion(f32[64,64,44,4,1]{1,2,4,3,0:T(8,128)} %fusion.105, f32[64,64,44,4,1]{1,2,4,3,0:T(8,128)} %fusion.108, bf16[64,14,4,64,1]{3,2,0,1,4:T(4,128)(2,1)} %bitcast.262, bf16[44,4,44,4]{2,0,1,3:T(8,128)(2,1)} %get-tuple-element.276), kind=kOutput, calls=%fused_computation.3.clone.1 | convolution fusion | flops 82903040 | bytes 15007744 | tf_op jit(solution)/shard_map/while/body/eval_jaxpr/niwpj,wpvq->nviqj/dot_general | solution.py:41
  539.7 5.2 copy.125
  555.7 4.6 fusion.105
  567.2 6.3 %fusion.110 = bf16[44,64,4,64]{3,0,2,1:T(8,128)(2,1)S(1)} fusion(f32[64,64,44,4,1]{1,2,4,3,0:T(8,128)} %fusion.105, f32[64,64,44,4,1]{1,2,4,3,0:T(8,128)} %fusion.108, bf16[64,14,4,64,1]{3,2,0,1,4:T(4,128)(2,1)} %bitcast.262, bf16[44,4,44,4]{2,0,1,3:T(8,128)(2,1)} %get-tuple-element.276), kind=kOutput, calls=%fused_computation.3.clone.1 | convolution fusion | flops 82903040 | bytes 15007744 | tf_op jit(solution)/shard_map/while/body/eval_jaxpr/niwpj,wpvq->nviqj/dot_general | solution.py:41
  573.5 5.2 copy.125
  589.5 4.6 fusion.105
  594.9 4.5 fusion.108
  601.0 6.3 %fusion.110 = bf16[44,64,4,64]{3,0,2,1:T(8,128)(2,1)S(1)} fusion(f32[64,64,44,4,1]{1,2,4,3,0:T(8,128)} %fusion.105, f32[64,64,44,4,1]{1,2,4,3,0:T(8,128)} %fusion.108, bf16[64,14,4,64,1]{3,2,0,1,4:T(4,128)(2,1)} %bitcast.262, bf16[44,4,44,4]{2,0,1,3:T(8,128)(2,1)} %get-tuple-element.276), kind=kOutput, calls=%fused_computation.3.clone.1 | convolution fusion | flops 82903040 | bytes 15007744 | tf_op jit(solution)/shard_map/while/body/eval_jaxpr/niwpj,wpvq->nviqj/dot_general | solution.py:41
  607.3 5.2 copy.125
  (386 shorter events, 209.8 us)
Async XLA Ops:
  6.5 57.2 %copy-start.4 = (bf16[8,16,2816]{2,1,0:T(8,128)(2,1)S(1)}, bf16[8,16,2816]{2,1,0:T(8,128)(2,1)}, u32[]{:S(2)}) copy-start(bf16[8,16,2816]{2,1,0:T(8,128)(2,1)} %param.13) | copy-start | bytes 2162692
  6.5 339.1 %all-gather.2.cloned.1.call-start = ((), (), s32[]{:S(2)}) async-start(), calls=%async_computation | async-start | bytes 3604480 | tf_op jit(solution)/shard_map/all_gather | solution.py:73
  6.5 20.3 %collective-permute-start.2 = (bf16[8,16,2816]{2,1,0:T(8,128)(2,1)}, bf16[8,16,2816]{2,1,0:T(8,128)(2,1)S(1)}, u32[]{:S(2)}, u32[]{:S(2)}) collective-permute-start(bf16[8,16,2816]{2,1,0:T(8,128)(2,1)} %param.13), channel_id=1, source_target_pairs={{0,8},{8,16},{16,24},{24,0},{1,9},{9,17},{17,25},{25,1},{2,10},{10... | collective-permute-start | bytes 2162696 | tf_op jit(solution)/shard_map/ppermute | solution.py:58
  26.8 18.2 %collective-permute-start.3 = (bf16[8,16,2816]{2,1,0:T(8,128)(2,1)S(1)}, bf16[8,16,2816]{2,1,0:T(8,128)(2,1)S(1)}, u32[]{:S(2)}, u32[]{:S(2)}) collective-permute-start(bf16[8,16,2816]{2,1,0:T(8,128)(2,1)S(1)} %collective-permute-done.2), channel_id=1, source_target_pairs={{0,8},{8,16},{16,24},{24,0},{1,9},{9,17},{17,25},{25,1},{2,10},{10... | collective-permute-start | bytes 2162696 | tf_op jit(solution)/shard_map/ppermute | solution.py:58
  45.1 17.4 %collective-permute-start.4 = (bf16[8,16,2816]{2,1,0:T(8,128)(2,1)S(1)}, bf16[8,16,2816]{2,1,0:T(8,128)(2,1)}, u32[]{:S(2)}, u32[]{:S(2)}) collective-permute-start(bf16[8,16,2816]{2,1,0:T(8,128)(2,1)S(1)} %collective-permute-done.3), channel_id=1, source_target_pairs={{0,8},{8,16},{16,24},{24,0},{1,9},{9,17},{17,25},{25,1},{2,10},{10... | collective-permute-start | bytes 2162696 | tf_op jit(solution)/shard_map/ppermute | solution.py:58
  45.9 9.5 %collective-permute-start.1 = (bf16[2,1,64,256]{3,2,1,0:T(8,128)(2,1)S(1)}, bf16[2,1,64,256]{3,2,1,0:T(8,128)(2,1)S(1)}, u32[]{:S(2)}, u32[]{:S(2)}) collective-permute-start(bf16[2,1,64,256]{3,2,1,0:T(8,128)(2,1)S(1)} %get-tuple-element.146), channel_id=1, source_target_pairs={{1,0},{2,1},{3,2},{4,3},{5,4},{6,5},{7,6},{9,8},{10,9},{11,10},{12... | collective-permute-start | bytes 196616 | tf_op jit(solution)/shard_map/ppermute | solution.py:16
  47.2 8.2 %collective-permute-start = (bf16[2,1,64,256]{3,2,1,0:T(8,128)(2,1)S(1)}, bf16[2,1,64,256]{3,2,1,0:T(8,128)(2,1)S(1)}, u32[]{:S(2)}, u32[]{:S(2)}) collective-permute-start(bf16[2,1,64,256]{3,2,1,0:T(8,128)(2,1)S(1)} %get-tuple-element.145), channel_id=1, source_target_pairs={{0,1},{1,2},{2,3},{3,4},{4,5},{5,6},{6,7},{8,9},{9,10},{10,11},{11... | collective-permute-start | bytes 196616 | tf_op jit(solution)/shard_map/ppermute | solution.py:15
  67.8 5.6 copy-start
  97.1 5.4 copy-start.1
  102.5 5.6 copy-start
  131.9 5.4 copy-start.1
  137.2 5.6 copy-start
  166.6 5.4 copy-start.1
  172.0 5.6 copy-start
  201.4 5.4 copy-start.1
  206.7 5.6 copy-start
  236.1 5.4 copy-start.1
  241.5 5.6 copy-start
  270.8 5.4 copy-start.1
  276.2 5.6 copy-start
  305.6 5.4 copy-start.1
  310.9 5.6 copy-start
  340.3 5.4 copy-start.1
  346.5 270.3 %copy-start.5 = (pred[8,256]{1,0:T(8,128)(4,1)S(1)}, pred[8,256]{1,0:T(8,128)(4,1)}, u32[]{:S(2)}) copy-start(pred[8,256]{1,0:T(8,128)(4,1)} %broadcast_compare_fusion) | copy-start | bytes 6148
  346.5 270.3 %copy-start.6 = (pred[8,64]{1,0:T(8,128)(4,1)S(1)}, pred[8,64]{1,0:T(8,128)(4,1)}, u32[]{:S(2)}) copy-start(pred[8,64]{1,0:T(8,128)(4,1)} %iota_compare_fusion) | copy-start | bytes 1540
  346.5 5.7 copy-start.2
  375.9 4.3 copy-start.3
  380.2 5.8 copy-start.2
  409.7 4.3 copy-start.3
  414.0 5.8 copy-start.2
  443.5 4.3 copy-start.3
  447.8 5.8 copy-start.2
  477.3 4.3 copy-start.3
  481.6 5.8 copy-start.2
  511.1 4.3 copy-start.3
  515.4 5.8 copy-start.2
  544.9 4.3 copy-start.3
  549.3 5.8 copy-start.2
  578.7 4.3 copy-start.3
  583.1 5.8 copy-start.2
  612.6 4.3 copy-start.3
Sparse Core Ops, SparseCore 0:
  50.4 43.3 all-gather.1
